TPU v7x, 32 devices: a whole 2x2x4 slice. The times are simulated.
32 devices in a mesh: lon: 4 (over x, core), frame: 8 (over z, y).
Axes of the slice: x: 2, y: 2, z: 4, core: 2. Of those that a mesh axis runs over, the one named last changes fastest.
Arguments:
- layer_input: bfloat16 [8, 16, 512, 128], P('frame', None, 'lon'), may hold values from -6 to 6
- hidden_saved: bfloat16 [8, 16, 512, 128], P('frame', None, 'lon'), as said below
- conv_weight: bfloat16 [3, 3, 128, 128], replicated, may hold values from -0.1875 to 0.1875
- queries: bfloat16 [2048, 128], P('lon'), may hold values from -6 to 6
- corr_cotangent: bfloat16 [8, 49, 2048], P('frame', None, 'lon'), may hold values from -0.59765625 to 0.59765625
- window_rows: int32 [8, 2048], P('frame', 'lon'), may hold values from 0 to 9
- window_cols: int32 [8, 2048], P('frame', 'lon'), may hold values from -3 to 124
- owner_strip: int32 [8, 2048, 1], P('frame', 'lon'), may hold values from 0 to 3; in each aligned block of 512 rows (0 to 511, 512 to 1023, ..., all dimensions but the last counted through in order) at most 128 rows name the same one
Outputs:
- query_grad: float32 [2048, 128], P(('lon', 'frame'))
- first_weight_grad: float32 [3, 3, 128, 128], replicated
- second_weight_grad: float32 [3, 3, 128, 128], replicated
Inputs may be any that keep to these rules, and one draw needn't show every extreme that they name: `hidden_saved`: rectifier outputs: zero or positive, a third or more of them exactly zero. `owner_strip`: in each frame, at most 128 of the 512 tracks homed on one strip name the same owning strip.
All inputs are finite; a program needn't handle non-finite values.
Results may differ from a plain program's by a relative error of at most 0.0045.
Values may be sent and summed in bfloat16 or wider, within the bound.
A program may use at most 64 MiB of HBM per device.

v0:
```python
import math
import jax
import jax.numpy as jnp
from jax import lax
from jax.sharding import PartitionSpec as P

WIN = 7


def padded_2(value, sides, width):
    for axis, dim in sides:
        peers, length = (lax.axis_size(axis), value.shape[dim])
        up = [(i, (i + 1) % peers) for i in range(peers)]
        down = [(j, i) for i, j in up]
        last = lax.slice_in_dim(value, length - width, length, axis=dim)
        first = lax.slice_in_dim(value, 0, width, axis=dim)
        before = lax.ppermute(last, axis, up)
        after = lax.ppermute(first, axis, down)
        value = jnp.concatenate([before, value, after], axis=dim)
    return value


def from_behind(value, axis, steps):
    count = lax.axis_size(axis)
    pairs = [(source, (source + steps) % count) for source in range(count)]
    return lax.ppermute(value, axis, pairs)


def pad_rows(field):
    return jnp.pad(field, ((1, 1), (0, 0), (0, 0)))


def conv_cells(padded, weight, out_cols):
    row_count = padded.shape[0] - 2
    result = jnp.zeros((row_count, out_cols, weight.shape[3]), jnp.float32)
    for row_tap in range(3):
        for col_tap in range(3):
            window = padded[row_tap : row_tap + row_count, col_tap : col_tap + out_cols]
            result = result + jnp.einsum(
                "rci,io->rco", window, weight[row_tap, col_tap], preferred_element_type=jnp.float32
            )
    return result


def conv_back(padded, weight, out_cols):
    row_count = padded.shape[0] - 2
    result = jnp.zeros((row_count, out_cols, weight.shape[2]), jnp.float32)
    for row_tap in range(3):
        for col_tap in range(3):
            window = padded[
                2 - row_tap : 2 - row_tap + row_count, 2 - col_tap : 2 - col_tap + out_cols
            ]
            result = result + jnp.einsum(
                "rco,io->rci", window, weight[row_tap, col_tap], preferred_element_type=jnp.float32
            )
    return result


def weight_terms(padded, grad):
    row_count, col_count, out_channels = grad.shape
    flat_grad = grad.reshape(row_count * col_count, out_channels)
    tap_terms = []
    for row_tap in range(3):
        for col_tap in range(3):
            window = padded[row_tap : row_tap + row_count, col_tap : col_tap + col_count].reshape(
                row_count * col_count, padded.shape[2]
            )
            tap_terms.append(
                lax.dot_general(
                    window, flat_grad, (((0,), (0,)), ((), ())), preferred_element_type=jnp.float32
                )
            )
    return jnp.stack(tap_terms).reshape(3, 3, padded.shape[2], out_channels)


def per_device(
    layer_input,
    hidden_saved,
    conv_weight,
    queries,
    corr_cotangent,
    window_rows,
    window_cols,
    owner_strip,
):
    strip_count = lax.axis_size("lon")
    input_local = layer_input[0]
    hidden_local = hidden_saved[0]
    row_count, col_count, channels = hidden_local.shape
    track_count = queries.shape[0]
    capacity = track_count // 4
    slot_count = strip_count * capacity
    wide_cols = col_count + 6
    taps_total = WIN * WIN
    reach = 4
    stacked = jnp.stack([input_local, hidden_local])
    edged = padded_2(stacked, (("lon", 2),), reach)
    input_edged = pad_rows(edged[0, :, reach - 1 : reach + col_count + 1])
    hidden_edged = pad_rows(edged[1, :, reach - 1 : reach + col_count + 1])
    feature_wide = conv_cells(pad_rows(edged[1]), conv_weight, wide_cols).astype(jnp.bfloat16)
    owners = owner_strip[0, :, 0]
    strip_ids = jnp.arange(strip_count, dtype=jnp.int32)
    marks = (owners[:, None] == strip_ids[None, :]).astype(jnp.int32)
    before = jnp.cumsum(marks, axis=0) - marks
    position = jnp.sum(before * marks, axis=1)
    slot_index = owners * capacity + position
    cot_rows = jnp.pad(corr_cotangent[0].T, ((0, 0), (0, 128 - taps_total)))
    meta_home = jnp.stack([window_rows[0], window_cols[0] + 3], axis=1)
    payload = jnp.concatenate([queries, cot_rows], axis=1)
    send_payload = (
        jnp.zeros((slot_count, payload.shape[1]), jnp.bfloat16).at[slot_index].set(payload)
    )
    send_meta = jnp.zeros((slot_count, meta_home.shape[1]), jnp.int32).at[slot_index].set(meta_home)
    got_payload, got_meta = (
        lax.all_to_all(send_payload, "lon", split_axis=0, concat_axis=0, tiled=True),
        lax.all_to_all(send_meta, "lon", split_axis=0, concat_axis=0, tiled=True),
    )
    query_slots = got_payload[:, :channels]
    cot_slots = got_payload[:, channels : channels + taps_total]
    block_rows = math.gcd(slot_count, 512)
    block_count = slot_count // block_rows
    feature_flat = feature_wide.reshape(row_count * wide_cols, channels)
    offsets = jnp.arange(WIN, dtype=jnp.int32)
    row_ids = jnp.arange(row_count, dtype=jnp.int32)
    col_ids = jnp.arange(wide_cols, dtype=jnp.int32)

    def block_step(grad_acc, block_items):
        cot_block, meta_block, query_block = block_items
        cot_square = cot_block.reshape(block_rows, WIN, WIN)
        row_hot = (
            meta_block[:, 0][:, None, None] + offsets[None, :, None] == row_ids[None, None, :]
        ).astype(jnp.bfloat16)
        col_hot = (
            meta_block[:, 1][:, None, None] + offsets[None, :, None] == col_ids[None, None, :]
        ).astype(jnp.bfloat16)
        placed_cols = jnp.einsum(
            "tij,tjh->tih", cot_square, col_hot, preferred_element_type=jnp.float32
        ).astype(jnp.bfloat16)
        spread = jnp.einsum(
            "tir,tih->trh", row_hot, placed_cols, preferred_element_type=jnp.float32
        ).astype(jnp.bfloat16)
        spread = spread.reshape(block_rows, row_count * wide_cols)
        block_grads = jnp.dot(spread, feature_flat, preferred_element_type=jnp.float32)
        grad_acc = grad_acc + lax.dot_general(
            spread, query_block, (((0,), (0,)), ((), ())), preferred_element_type=jnp.float32
        )
        return (grad_acc, block_grads)

    block_items = (
        cot_slots.reshape(block_count, block_rows, taps_total),
        got_meta.reshape(block_count, block_rows, got_meta.shape[1]),
        query_slots.reshape(block_count, block_rows, channels),
    )
    grad_flat, query_blocks = lax.scan(
        block_step, jnp.zeros((row_count * wide_cols, channels), jnp.float32), block_items
    )
    slot_grads = query_blocks.reshape(slot_count, channels)
    returned = lax.all_to_all(slot_grads, "lon", split_axis=0, concat_axis=0, tiled=True)
    home_grads = returned[slot_index]
    query_grad = lax.psum_scatter(home_grads, "frame", scatter_dimension=0, tiled=True)
    grad_wide = grad_flat.reshape(row_count, wide_cols, channels)
    from_prior = from_behind(grad_wide[:, col_count + 3 :], "lon", 1)
    from_next = from_behind(grad_wide[:, :3], "lon", -1)
    own_grad = grad_wide[:, 3 : col_count + 3]
    own_grad = own_grad.at[:, :3].add(from_prior)
    own_grad = own_grad.at[:, col_count - 3 :].add(from_next)
    grad_edged = padded_2(own_grad.astype(jnp.bfloat16), (("lon", 1),), 1)
    feature_grad = grad_edged[:, 1 : col_count + 1]
    hidden_grad = conv_back(pad_rows(grad_edged), conv_weight, col_count)
    pre_grad = jnp.where(hidden_local > 0, hidden_grad, jnp.zeros_like(hidden_grad)).astype(
        jnp.bfloat16
    )
    second_term = weight_terms(hidden_edged, feature_grad)
    first_term = weight_terms(input_edged, pre_grad)
    first_sum, second_sum = lax.psum((first_term, second_term), ("lon", "frame"))
    norm_factor = 1.0 / math.sqrt(row_count * col_count * strip_count * lax.axis_size("frame"))
    return (query_grad, first_sum * norm_factor, second_sum * norm_factor)


def solution(mesh):
    placed = (
        P("frame", None, "lon", None),
        P("frame", None, "lon", None),
        P(),
        P("lon", None),
        P("frame", None, "lon"),
        P("frame", "lon"),
        P("frame", "lon"),
        P("frame", "lon", None),
    )
    return jax.shard_map(
        per_device,
        mesh=mesh,
        in_specs=placed,
        out_specs=(P(("lon", "frame"), None), P(), P()),
        check_vma=False,
    )
```

profile of v0, /device:TPU:0, one launch (start us, length us, event | category | flops | bytes accessed | tf_op | source)
XLA Modules:
  0.0 221.2 jit_solution(16327299058159711779)
XLA Ops:
  8.8 1.2 reduce-window.6
  13.4 1.8 scatter_custom_fusion
  15.9 4.2 %all-to-all-start = ((s32[4,128,2]{1,2,0:T(2,128)}), s32[4,128,2]{1,2,0:T(2,128)S(1)}, u32[]{:S(2)}, u32[]{:S(2)}) async-start(s32[4,128,2]{1,2,0:T(2,128)} %copy.76), calls=%async_computation | async-start | bytes 8192 | tf_op jit(solution)/shard_map/all_to_all | solution.py:116
  20.3 1.8 collective-permute-start.1
  22.4 3.0 %scatter_custom_fusion.1 = bf16[512,256]{1,0:T(8,128)(2,1)} fusion(s32[512]{0:T(512)S(1)} %bitcast.248, bf16[512,256]{1,0:T(8,128)(2,1)S(1)} %copy.78, bf16[]{:T(256)} %constant.86.clone.1), kind=kCustom, calls=%fused_computation.147 | custom fusion | bytes 262146 | tf_op jit(solution)/shard_map/scatter | solution.py:111
  25.4 3.4 %all-to-all-start.1 = ((bf16[4,128,256]{2,1,0:T(8,128)(2,1)}), bf16[4,128,256]{2,1,0:T(8,128)(2,1)S(1)}, u32[]{:S(2)}, u32[]{:S(2)}) async-start(bf16[4,128,256]{2,1,0:T(8,128)(2,1)} %bitcast.13), calls=%async_computation.1 | async-start | bytes 524288 | tf_op jit(solution)/shard_map/all_to_all | solution.py:115
  29.9 0.9 copy-done.3
  34.2 1.3 fusion.9
  36.1 5.9 %fusion.1 = bf16[512,16,134]{2,1,0:T(8,128)(2,1)} fusion(bf16[512,7,7]{2,1,0:T(8,128)(2,1)S(1)} %reshape.292, s32[512,7]{1,0:T(8,128)S(1)} %get-tuple-element.69, s32[512,7]{1,0:T(8,128)S(1)} %get-tuple-element.70), kind=kOutput, calls=%fused_computation.5 | convolution fusion | flops 23109632 | bytes 2274304 | tf_op jit(solution)/shard_map/while/body/eval_jaxpr/tir,tih->trh/dot_general | solution.py:139
  42.0 7.9 %copy.81 = bf16[512,16,134]{0,1,2:T(8,128)(2,1)} copy(bf16[512,16,134]{2,1,0:T(8,128)(2,1)} %fusion.1) | data formatting | bytes 4390912 | tf_op jit(solution)/shard_map/while/body/eval_jaxpr/tir,tih->trh/dot_general | solution.py:139
  49.9 2.8 %copy.83 = bf16[512,16,134]{0,2,1:T(8,128)(2,1)S(1)} copy(bf16[512,16,134]{0,1,2:T(8,128)(2,1)} %copy.81) | data formatting | bytes 4390912 | tf_op jit(solution)/shard_map/while/body/eval_jaxpr/convert_element_type | solution.py:141
  52.7 2.1 reshape.236
  54.9 2.6 %dot_general.141 = bf16[16,134,512]{2,1,0:T(8,128)(2,1)S(1)} reshape(bf16[2144,512]{1,0:T(8,128)(2,1)} %bitcast.235) | data formatting | bytes 4390912 | tf_op jit(solution)/shard_map/while/body/eval_jaxpr/dot_general | solution.py:144
  57.5 1.6 fusion.97
  60.2 1.3 collective-permute-start.3
  61.5 1.1 collective-permute-done.2
  63.7 1.8 collective-permute-start.5
  77.5 2.5 %fusion.46 = f32[512,128,1]{1,0,2:T(8,128)} fusion(bf16[512,16,134]{0,1,2:T(8,128)(2,1)S(1)} %copy-done, bf16[16,134,128]{2,1,0:T(8,128)(2,1)} %fusion.9), kind=kOutput, calls=%fused_computation.87 | convolution fusion | flops 281018368 | bytes 3006464 | tf_op jit(solution)/shard_map/while/body/eval_jaxpr/dot_general | solution.py:143
  80.0 3.4 %all-to-all-start.2 = ((f32[4,128,128]{2,1,0:T(8,128)}), f32[4,128,128]{2,1,0:T(8,128)S(1)}, u32[]{:S(2)}, u32[]{:S(2)}) async-start(f32[4,128,128]{2,1,0:T(8,128)} %bitcast.36), calls=%async_computation.2 | async-start | bytes 524288 | tf_op jit(solution)/shard_map/all_to_all | solution.py:158
  83.5 6.6 %all-to-all-done.2 = f32[4,128,128]{2,1,0:T(8,128)S(1)} async-done(((f32[4,128,128]{2,1,0:T(8,128)}), f32[4,128,128]{2,1,0:T(8,128)S(1)}, u32[]{:S(2)}, u32[]{:S(2)}) %all-to-all-start.2) | async-done | bytes 262176 | tf_op jit(solution)/shard_map/all_to_all | solution.py:158
  90.1 1.6 gather_fusion
  91.8 119.1 %all-reduce.8.cloned.1.call-done = (f32[3,3,128,128]{3,2,1,0:T(8,128)}, f32[3,3,128,128]{3,2,1,0:T(8,128)}) async-done(((f32[3,3,128,128]{3,2,1,0:T(8,128)}, f32[3,3,128,128]{3,2,1,0:T(8,128)}), (f32[3,3,128,128]{3,2,1,0:T(8,128)}, f32[3,3,128,128]{3,2,1,0:T(8,128)})) %all-reduce.8.cloned.1.call-update) | async-done | bytes 1179664 | tf_op jit(solution)/shard_map/psum | solution.py:175
  210.9 2.0 broadcast_multiply_fusion.1
  212.9 0.9 broadcast_multiply_fusion
  (106 shorter events, 24.3 us)
Async XLA Ops:
  8.0 12.1 %copy-start.9 = (bf16[1,16,128,128]{3,2,1,0:T(8,128)(2,1)S(1)}, bf16[1,16,128,128]{3,2,1,0:T(8,128)(2,1)}, u32[]{:S(2)}) copy-start(bf16[1,16,128,128]{3,2,1,0:T(8,128)(2,1)} %param.12) | copy-start | bytes 1572868
  8.0 12.2 %copy-start.1 = (bf16[1,16,128,128]{3,2,1,0:T(8,128)(2,1)S(1)}, bf16[1,16,128,128]{3,2,1,0:T(8,128)(2,1)}, u32[]{:S(2)}) copy-start(bf16[1,16,128,128]{3,2,1,0:T(8,128)(2,1)} %param.13) | copy-start | bytes 1572868
  15.9 9.5 %all-to-all-start = ((s32[4,128,2]{1,2,0:T(2,128)}), s32[4,128,2]{1,2,0:T(2,128)S(1)}, u32[]{:S(2)}, u32[]{:S(2)}) async-start(s32[4,128,2]{1,2,0:T(2,128)} %copy.76), calls=%async_computation | async-start | bytes 8192 | tf_op jit(solution)/shard_map/all_to_all | solution.py:116
  20.1 2.0 copy-start.10
  20.1 2.1 copy-start.11
  20.3 9.0 %collective-permute-start.1 = (bf16[2,16,4,128]{3,2,1,0:T(4,128)(2,1)S(1)}, bf16[2,16,4,128]{3,2,1,0:T(4,128)(2,1)S(1)}, u32[]{:S(2)}, u32[]{:S(2)}) collective-permute-start(bf16[2,16,4,128]{3,2,1,0:T(4,128)(2,1)S(1)} %get-tuple-element.64), channel_id=1, source_target_pairs={{8,0},{16,8},{24,16},{0,24},{9,1},{17,9},{25,17},{1,25},{10,2},{18... | collective-permute-start | bytes 98312 | tf_op jit(solution)/shard_map/ppermute | solution.py:18
  22.1 7.2 %collective-permute-start = (bf16[2,16,4,128]{3,2,1,0:T(4,128)(2,1)S(1)}, bf16[2,16,4,128]{3,2,1,0:T(4,128)(2,1)S(1)}, u32[]{:S(2)}, u32[]{:S(2)}) collective-permute-start(bf16[2,16,4,128]{3,2,1,0:T(4,128)(2,1)S(1)} %get-tuple-element.63), channel_id=1, source_target_pairs={{0,8},{8,16},{16,24},{24,0},{1,9},{9,17},{17,25},{25,1},{2,10},{10... | collective-permute-start | bytes 98312 | tf_op jit(solution)/shard_map/ppermute | solution.py:17
  25.4 10.1 %all-to-all-start.1 = ((bf16[4,128,256]{2,1,0:T(8,128)(2,1)}), bf16[4,128,256]{2,1,0:T(8,128)(2,1)S(1)}, u32[]{:S(2)}, u32[]{:S(2)}) async-start(bf16[4,128,256]{2,1,0:T(8,128)(2,1)} %bitcast.13), calls=%async_computation.1 | async-start | bytes 524288 | tf_op jit(solution)/shard_map/all_to_all | solution.py:115
  28.8 182.1 %all-reduce.8.cloned.1.call-start = ((), (), s32[]{:S(2)}) async-start(), calls=%async_computation.5 | async-start | bytes 2359296 | tf_op jit(solution)/shard_map/psum | solution.py:175
  29.8 1.0 copy-start.3
  35.5 6.5 %copy-start.5 = (bf16[4,128,256]{2,1,0:T(8,128)(2,1)}, bf16[4,128,256]{2,1,0:T(8,128)(2,1)S(1)}, u32[]{:S(2)}) copy-start(bf16[4,128,256]{2,1,0:T(8,128)(2,1)S(1)} %all-to-all-done.1) | copy-start | bytes 786436
  59.2 3.4 %collective-permute-start.2 = (f32[16,3,128]{2,1,0:T(4,128)S(1)}, f32[16,3,128]{2,1,0:T(4,128)S(1)}, u32[]{:S(2)}, u32[]{:S(2)}) collective-permute-start(f32[16,3,128]{2,1,0:T(4,128)S(1)} %get-tuple-element.62), channel_id=1, source_target_pairs={{0,8},{8,16},{16,24},{24,0},{1,9},{9,17},{17,25},{25,1},{2,10},{10... | collective-permute-start | bytes 73736 | tf_op jit(solution)/shard_map/ppermute | solution.py:26
  60.2 3.2 %copy-start.4 = (bf16[3,3,128,128]{3,2,1,0:T(8,128)(2,1)S(1)}, bf16[3,3,128,128]{3,2,1,0:T(8,128)(2,1)}, u32[]{:S(2)}) copy-start(bf16[3,3,128,128]{3,2,1,0:T(8,128)(2,1)} %param.14) | copy-start | bytes 884740
  60.2 2.9 %collective-permute-start.3 = (f32[16,3,128]{2,1,0:T(4,128)S(1)}, f32[16,3,128]{2,1,0:T(4,128)S(1)}, u32[]{:S(2)}, u32[]{:S(2)}) collective-permute-start(f32[16,3,128]{2,1,0:T(4,128)S(1)} %get-tuple-element.61), channel_id=1, source_target_pairs={{0,24},{8,0},{16,8},{24,16},{1,25},{9,1},{17,9},{25,17},{2,26},{10... | collective-permute-start | bytes 73736 | tf_op jit(solution)/shard_map/ppermute | solution.py:26
  63.7 5.4 %collective-permute-start.5 = (bf16[16,1,128]{2,1,0:T(2,128)(2,1)S(1)}, bf16[16,1,128]{2,1,0:T(2,128)(2,1)S(1)}, u32[]{:S(2)}, u32[]{:S(2)}) collective-permute-start(bf16[16,1,128]{2,1,0:T(2,128)(2,1)S(1)} %get-tuple-element.66), channel_id=1, source_target_pairs={{8,0},{16,8},{24,16},{0,24},{9,1},{17,9},{25,17},{1,25},{10,2},{18... | collective-permute-start | bytes 12296 | tf_op jit(solution)/shard_map/ppermute | solution.py:18
  65.5 3.6 %collective-permute-start.4 = (bf16[16,1,128]{2,1,0:T(2,128)(2,1)S(1)}, bf16[16,1,128]{2,1,0:T(2,128)(2,1)S(1)}, u32[]{:S(2)}, u32[]{:S(2)}) collective-permute-start(bf16[16,1,128]{2,1,0:T(2,128)(2,1)S(1)} %get-tuple-element.65), channel_id=1, source_target_pairs={{0,8},{8,16},{16,24},{24,0},{1,9},{9,17},{17,25},{25,1},{2,10},{10... | collective-permute-start | bytes 12296 | tf_op jit(solution)/shard_map/ppermute | solution.py:17
  69.1 0.8 copy-start.6
  71.5 1.0 copy-start.2
  75.6 1.8 copy-start
  76.0 0.8 copy-start.7
  80.0 10.1 %all-to-all-start.2 = ((f32[4,128,128]{2,1,0:T(8,128)}), f32[4,128,128]{2,1,0:T(8,128)S(1)}, u32[]{:S(2)}, u32[]{:S(2)}) async-start(f32[4,128,128]{2,1,0:T(8,128)} %bitcast.36), calls=%async_computation.2 | async-start | bytes 524288 | tf_op jit(solution)/shard_map/all_to_all | solution.py:158
  83.4 130.3 %reduce-scatter.2.cloned.1.call-start = ((), (), s32[]{:S(2)}) async-start(), calls=%async_computation.4 | async-start | bytes 294912 | tf_op jit(solution)/shard_map/reduce_scatter | solution.py:160
  210.9 2.0 copy-start.8
Sparse Core Ops, SparseCore 0:
  77.0 133.8 all-reduce.7
Sparse Core Ops, SparseCore 1:
  91.8 62.9 reduce-scatter.1
where the time goes:
time: 222 us; the launch traced here: 221 us
  waiting for transfers between devices  127 us (57%)
  local copies, waits for them, and re-layouts  28.2 us (13%)
  matrix products  23.8 us (11%)
  starting transfers between devices  17.2 us (8%)
  between operations  16 us (7%)
  other arithmetic  8.87 us (4%)
    psum x1, waiting for transfers between devices, per_device(): lax.psum((first_term, second_term), ('lon', 'frame'))  119 us
    dot_general x1, local copies, waits for them, and re-layouts, block_step(): jnp.einsum('tir,tih->trh', row_hot, placed_cols, preferred_element_type=j...  7.86 us
    all_to_all x1, waiting for transfers between devices, per_device(): lax.all_to_all(slot_grads, 'lon', split_axis=0, concat_axis=0, tiled=True)  6.61 us
    dot_general x18, matrix products, weight_terms(): lax.dot_general(window, flat_grad, (((0,), (0,)), ((), ())), preferred_el...  6.16 us
    dot_general x1, matrix products, block_step(): jnp.einsum('tir,tih->trh', row_hot, placed_cols, preferred_element_type=j...  5.92 us
    dot_general x9, matrix products, conv_cells(): jnp.einsum('rci,io->rco', window, weight[row_tap, col_tap], preferred_ele...  4.72 us
  transfers between devices with their start and end apart: 11, of which 4 were waited for; matrix products, arithmetic and copies ran while one was open for 9% of the time, Pallas kernels for 0%

commit v1 on v0

--- a/solution.py
+++ b/solution.py
@@ -172,7 +172,7 @@
     )
     second_term = weight_terms(hidden_edged, feature_grad)
     first_term = weight_terms(input_edged, pre_grad)
-    first_sum, second_sum = lax.psum((first_term, second_term), ("lon", "frame"))
+    first_sum, second_sum = lax.psum(lax.psum((first_term, second_term), "lon"), "frame")
     norm_factor = 1.0 / math.sqrt(row_count * col_count * strip_count * lax.axis_size("frame"))
     return (query_grad, first_sum * norm_factor, second_sum * norm_factor)
 

time: 222 us -> 276 us (1.24)
  waiting for transfers between devices: 127 us -> 177 us
    reduce_scatter x1, waiting for transfers between devices: 0.01 us -> 62.3 us  [per_device(): lax.psum_scatter(home_grads, 'frame', scatter_dimension=0, tiled=True)]
    psum x1 -> x2, waiting for transfers between devices: 119 us -> 108 us  [the longest x1 69.5 us: per_device(): lax.psum(lax.psum((first_term, second_term), 'lon'), 'frame')]
    dot_general x9, matrix products: 4.72 us -> 7.95 us  [conv_cells(): jnp.einsum('rci,io->rco', window, weight[row_tap, col_tap], preferred_ele...]
  transfers between devices with their start and end apart: 11 -> 12, of which waited for: 4 -> 5; matrix products, arithmetic and copies ran while one was open for 9% -> 8% of each run, Pallas kernels for 0% -> 0%
where the time goes in v1:
time: 276 us; the launch traced here: 274 us
  waiting for transfers between devices  177 us (64%)
  local copies, waits for them, and re-layouts  29.1 us (11%)
  matrix products  26.2 us (9%)
  starting transfers between devices  16.6 us (6%)
  between operations  14.3 us (5%)
  other arithmetic  10.9 us (4%)
    psum x1, waiting for transfers between devices, per_device(): lax.psum(lax.psum((first_term, second_term), 'lon'), 'frame')  69.5 us
    reduce_scatter x1, waiting for transfers between devices, per_device(): lax.psum_scatter(home_grads, 'frame', scatter_dimension=0, tiled=True)  62.3 us
    psum x1, waiting for transfers between devices, per_device(): lax.psum((first_term, second_term), 'lon')  38.5 us
    dot_general x9, matrix products, conv_cells(): jnp.einsum('rci,io->rco', window, weight[row_tap, col_tap], preferred_ele...  7.95 us
    dot_general x1, local copies, waits for them, and re-layouts, block_step(): jnp.einsum('tir,tih->trh', row_hot, placed_cols, preferred_element_type=j...  7.86 us
    dot_general x18, matrix products, weight_terms(): lax.dot_general(window, flat_grad, (((0,), (0,)), ((), ())), preferred_el...  6.14 us
    all_to_all x1, waiting for transfers between devices, per_device(): lax.all_to_all(slot_grads, 'lon', split_axis=0, concat_axis=0, tiled=True)  5.91 us
    dot_general x1, matrix products, block_step(): jnp.einsum('tir,tih->trh', row_hot, placed_cols, preferred_element_type=j...  5.91 us
  transfers between devices with their start and end apart: 12, of which 5 were waited for; matrix products, arithmetic and copies ran while one was open for 8% of the time, Pallas kernels for 0%

profile of v1, /device:TPU:0, one launch (start us, length us, event | category | flops | bytes accessed | tf_op | source)
XLA Modules:
  0.0 274.2 jit_solution(12328404594848795233)
XLA Ops:
  8.0 1.2 reduce-window.6
  12.6 1.8 scatter_custom_fusion
  15.1 4.2 %all-to-all-start = ((s32[4,128,2]{1,2,0:T(2,128)}), s32[4,128,2]{1,2,0:T(2,128)S(1)}, u32[]{:S(2)}, u32[]{:S(2)}) async-start(s32[4,128,2]{1,2,0:T(2,128)} %copy.76), calls=%async_computation | async-start | bytes 8192 | tf_op jit(solution)/shard_map/all_to_all | solution.py:116
  19.5 1.8 collective-permute-start.1
  21.6 3.0 %scatter_custom_fusion.1 = bf16[512,256]{1,0:T(8,128)(2,1)} fusion(s32[512]{0:T(512)S(1)} %bitcast.248, bf16[512,256]{1,0:T(8,128)(2,1)S(1)} %copy.78, bf16[]{:T(256)} %constant.86.clone.1), kind=kCustom, calls=%fused_computation.147 | custom fusion | bytes 262146 | tf_op jit(solution)/shard_map/scatter | solution.py:111
  24.6 3.4 %all-to-all-start.1 = ((bf16[4,128,256]{2,1,0:T(8,128)(2,1)}), bf16[4,128,256]{2,1,0:T(8,128)(2,1)S(1)}, u32[]{:S(2)}, u32[]{:S(2)}) async-start(bf16[4,128,256]{2,1,0:T(8,128)(2,1)} %bitcast.13), calls=%async_computation.1 | async-start | bytes 524288 | tf_op jit(solution)/shard_map/all_to_all | solution.py:115
  32.5 2.2 convolution_add_fusion.5
  35.3 5.9 %fusion.1 = bf16[512,16,134]{2,1,0:T(8,128)(2,1)} fusion(bf16[512,7,7]{2,1,0:T(8,128)(2,1)S(1)} %reshape.292, s32[512,7]{1,0:T(8,128)S(1)} %get-tuple-element.71, s32[512,7]{1,0:T(8,128)S(1)} %get-tuple-element.72), kind=kOutput, calls=%fused_computation.5 | convolution fusion | flops 23109632 | bytes 2274304 | tf_op jit(solution)/shard_map/while/body/eval_jaxpr/tir,tih->trh/dot_general | solution.py:139
  41.2 7.9 %copy.81 = bf16[512,16,134]{0,1,2:T(8,128)(2,1)} copy(bf16[512,16,134]{2,1,0:T(8,128)(2,1)} %fusion.1) | data formatting | bytes 4390912 | tf_op jit(solution)/shard_map/while/body/eval_jaxpr/tir,tih->trh/dot_general | solution.py:139
  49.0 2.8 %copy.83 = bf16[512,16,134]{0,2,1:T(8,128)(2,1)S(1)} copy(bf16[512,16,134]{0,1,2:T(8,128)(2,1)} %copy.81) | data formatting | bytes 4390912 | tf_op jit(solution)/shard_map/while/body/eval_jaxpr/convert_element_type | solution.py:141
  51.9 2.1 reshape.236
  54.0 2.6 dot_general.141
  56.6 1.7 fusion.97
  60.0 1.5 collective-permute-start.3
  63.9 1.4 slice_add_fusion
  66.6 1.3 collective-permute-start.5
  79.9 38.5 %all-reduce.12.cloned.1.call-done = (f32[3,3,128,128]{3,2,1,0:T(8,128)}, f32[3,3,128,128]{3,2,1,0:T(8,128)}) async-done(((f32[3,3,128,128]{3,2,1,0:T(8,128)}, f32[3,3,128,128]{3,2,1,0:T(8,128)}), (f32[3,3,128,128]{3,2,1,0:T(8,128)}, f32[3,3,128,128]{3,2,1,0:T(8,128)})) %all-reduce.12.cloned.1.call-update) | async-done | bytes 1179664 | tf_op jit(solution)/shard_map/psum | solution.py:175
  120.5 1.5 fusion.46
  122.0 3.4 %all-to-all-start.2 = ((f32[4,128,128]{2,1,0:T(8,128)}), f32[4,128,128]{2,1,0:T(8,128)S(1)}, u32[]{:S(2)}, u32[]{:S(2)}) async-start(f32[4,128,128]{2,1,0:T(8,128)} %bitcast.36), calls=%async_computation.2 | async-start | bytes 524288 | tf_op jit(solution)/shard_map/all_to_all | solution.py:158
  125.5 5.9 %all-to-all-done.2 = f32[4,128,128]{2,1,0:T(8,128)S(1)} async-done(((f32[4,128,128]{2,1,0:T(8,128)}), f32[4,128,128]{2,1,0:T(8,128)S(1)}, u32[]{:S(2)}, u32[]{:S(2)}) %all-to-all-start.2) | async-done | bytes 262176 | tf_op jit(solution)/shard_map/all_to_all | solution.py:158
  131.4 1.6 gather_fusion
  133.0 69.5 %all-reduce.10.cloned.1.call-done = (f32[3,3,128,128]{3,2,1,0:T(8,128)}, f32[3,3,128,128]{3,2,1,0:T(8,128)}) async-done(((f32[3,3,128,128]{3,2,1,0:T(8,128)}, f32[3,3,128,128]{3,2,1,0:T(8,128)}), (f32[3,3,128,128]{3,2,1,0:T(8,128)}, f32[3,3,128,128]{3,2,1,0:T(8,128)})) %all-reduce.10.cloned.1.call-update) | async-done | bytes 1179664 | tf_op jit(solution)/shard_map/psum | solution.py:175
  202.5 2.0 broadcast_multiply_fusion.1
  205.3 62.3 %reduce-scatter.2.cloned.1.call-done = f32[64,128]{1,0:T(8,128)} async-done(((f32[512,128]{1,0:T(8,128)}), f32[64,128]{1,0:T(8,128)}) %reduce-scatter.2.cloned.1.call-update) | async-done | bytes 32784 | tf_op jit(solution)/shard_map/reduce_scatter | solution.py:160
  (111 shorter events, 30.4 us)
Async XLA Ops:
  7.2 12.1 %copy-start.10 = (bf16[1,16,128,128]{3,2,1,0:T(8,128)(2,1)S(1)}, bf16[1,16,128,128]{3,2,1,0:T(8,128)(2,1)}, u32[]{:S(2)}) copy-start(bf16[1,16,128,128]{3,2,1,0:T(8,128)(2,1)} %param.12) | copy-start | bytes 1572868
  7.2 12.2 %copy-start.4 = (bf16[1,16,128,128]{3,2,1,0:T(8,128)(2,1)S(1)}, bf16[1,16,128,128]{3,2,1,0:T(8,128)(2,1)}, u32[]{:S(2)}) copy-start(bf16[1,16,128,128]{3,2,1,0:T(8,128)(2,1)} %param.13) | copy-start | bytes 1572868
  15.1 9.5 %all-to-all-start = ((s32[4,128,2]{1,2,0:T(2,128)}), s32[4,128,2]{1,2,0:T(2,128)S(1)}, u32[]{:S(2)}, u32[]{:S(2)}) async-start(s32[4,128,2]{1,2,0:T(2,128)} %copy.76), calls=%async_computation | async-start | bytes 8192 | tf_op jit(solution)/shard_map/all_to_all | solution.py:116
  19.3 2.0 copy-start.11
  19.3 2.1 copy-start.12
  19.5 8.8 %collective-permute-start.1 = (bf16[2,16,4,128]{3,2,1,0:T(4,128)(2,1)S(1)}, bf16[2,16,4,128]{3,2,1,0:T(4,128)(2,1)S(1)}, u32[]{:S(2)}, u32[]{:S(2)}) collective-permute-start(bf16[2,16,4,128]{3,2,1,0:T(4,128)(2,1)S(1)} %get-tuple-element.66), channel_id=1, source_target_pairs={{8,0},{16,8},{24,16},{0,24},{9,1},{17,9},{25,17},{1,25},{10,2},{18... | collective-permute-start | bytes 98312 | tf_op jit(solution)/shard_map/ppermute | solution.py:18
  21.3 7.0 %collective-permute-start = (bf16[2,16,4,128]{3,2,1,0:T(4,128)(2,1)S(1)}, bf16[2,16,4,128]{3,2,1,0:T(4,128)(2,1)S(1)}, u32[]{:S(2)}, u32[]{:S(2)}) collective-permute-start(bf16[2,16,4,128]{3,2,1,0:T(4,128)(2,1)S(1)} %get-tuple-element.65), channel_id=1, source_target_pairs={{0,8},{8,16},{16,24},{24,0},{1,9},{9,17},{17,25},{25,1},{2,10},{10... | collective-permute-start | bytes 98312 | tf_op jit(solution)/shard_map/ppermute | solution.py:17
  24.6 10.1 %all-to-all-start.1 = ((bf16[4,128,256]{2,1,0:T(8,128)(2,1)}), bf16[4,128,256]{2,1,0:T(8,128)(2,1)S(1)}, u32[]{:S(2)}, u32[]{:S(2)}) async-start(bf16[4,128,256]{2,1,0:T(8,128)(2,1)} %bitcast.13), calls=%async_computation.1 | async-start | bytes 524288 | tf_op jit(solution)/shard_map/all_to_all | solution.py:115
  28.0 90.4 %all-reduce.12.cloned.1.call-start = ((), (), s32[]{:S(2)}) async-start(), calls=%async_computation.6 | async-start | bytes 2359296 | tf_op jit(solution)/shard_map/psum | solution.py:175
  28.8 1.3 copy-start.1
  34.6 6.5 %copy-start.6 = (bf16[4,128,256]{2,1,0:T(8,128)(2,1)}, bf16[4,128,256]{2,1,0:T(8,128)(2,1)S(1)}, u32[]{:S(2)}) copy-start(bf16[4,128,256]{2,1,0:T(8,128)(2,1)S(1)} %all-to-all-done.1) | copy-start | bytes 786436
  56.6 2.9 %copy-start.2 = (bf16[2,16,136,128]{3,2,1,0:T(8,128)(2,1)S(1)}, bf16[2,16,136,128]{3,2,1,0:T(8,128)(2,1)}, u32[]{:S(2)}) copy-start(bf16[2,16,136,128]{3,2,1,0:T(8,128)(2,1)} %copy-done.1) | copy-start | bytes 3342340
  59.0 3.3 %collective-permute-start.2 = (f32[16,3,128]{2,1,0:T(4,128)S(1)}, f32[16,3,128]{2,1,0:T(4,128)S(1)}, u32[]{:S(2)}, u32[]{:S(2)}) collective-permute-start(f32[16,3,128]{2,1,0:T(4,128)S(1)} %get-tuple-element.64), channel_id=1, source_target_pairs={{0,8},{8,16},{16,24},{24,0},{1,9},{9,17},{17,25},{25,1},{2,10},{10... | collective-permute-start | bytes 73736 | tf_op jit(solution)/shard_map/ppermute | solution.py:26
  60.0 6.3 %copy-start.5 = (bf16[3,3,128,128]{3,2,1,0:T(8,128)(2,1)S(1)}, bf16[3,3,128,128]{3,2,1,0:T(8,128)(2,1)}, u32[]{:S(2)}) copy-start(bf16[3,3,128,128]{3,2,1,0:T(8,128)(2,1)} %param.14) | copy-start | bytes 884740
  60.0 3.9 %collective-permute-start.3 = (f32[16,3,128]{2,1,0:T(4,128)}, f32[16,3,128]{2,1,0:T(4,128)}, u32[]{:S(2)}, u32[]{:S(2)}) collective-permute-start(f32[16,3,128]{2,1,0:T(4,128)} %get-tuple-element.63), channel_id=1, source_target_pairs={{0,24},{8,0},{16,8},{24,16},{1,25},{9,1},{17,9},{25,17},{2,26},{10... | collective-permute-start | bytes 73736 | tf_op jit(solution)/shard_map/ppermute | solution.py:26
  66.6 4.8 %collective-permute-start.5 = (bf16[16,1,128]{2,1,0:T(2,128)(2,1)S(1)}, bf16[16,1,128]{2,1,0:T(2,128)(2,1)S(1)}, u32[]{:S(2)}, u32[]{:S(2)}) collective-permute-start(bf16[16,1,128]{2,1,0:T(2,128)(2,1)S(1)} %get-tuple-element.68), channel_id=1, source_target_pairs={{8,0},{16,8},{24,16},{0,24},{9,1},{17,9},{25,17},{1,25},{10,2},{18... | collective-permute-start | bytes 12296 | tf_op jit(solution)/shard_map/ppermute | solution.py:18
  67.9 3.5 %collective-permute-start.4 = (bf16[16,1,128]{2,1,0:T(2,128)(2,1)S(1)}, bf16[16,1,128]{2,1,0:T(2,128)(2,1)S(1)}, u32[]{:S(2)}, u32[]{:S(2)}) collective-permute-start(bf16[16,1,128]{2,1,0:T(2,128)(2,1)S(1)} %get-tuple-element.67), channel_id=1, source_target_pairs={{0,8},{8,16},{16,24},{24,0},{1,9},{9,17},{17,25},{25,1},{2,10},{10... | collective-permute-start | bytes 12296 | tf_op jit(solution)/shard_map/ppermute | solution.py:17
  71.4 0.8 copy-start.7
  77.3 1.3 copy-start.3
  78.5 124.0 %all-reduce.10.cloned.1.call-start = ((), (), s32[]{:S(2)}) async-start(), calls=%async_computation.5 | async-start | bytes 2359296 | tf_op jit(solution)/shard_map/psum | solution.py:175
  118.9 1.6 copy-start
  122.0 9.4 %all-to-all-start.2 = ((f32[4,128,128]{2,1,0:T(8,128)}), f32[4,128,128]{2,1,0:T(8,128)S(1)}, u32[]{:S(2)}, u32[]{:S(2)}) async-start(f32[4,128,128]{2,1,0:T(8,128)} %bitcast.36), calls=%async_computation.2 | async-start | bytes 524288 | tf_op jit(solution)/shard_map/all_to_all | solution.py:158
  125.4 142.3 %reduce-scatter.2.cloned.1.call-start = ((), (), s32[]{:S(2)}) async-start(), calls=%async_computation.4 | async-start | bytes 294912 | tf_op jit(solution)/shard_map/reduce_scatter | solution.py:160
  202.5 2.0 copy-start.9
  (1 other events, 0.8 us)
Sparse Core Ops, SparseCore 0:
  78.6 39.7 all-reduce.11
  121.9 80.5 all-reduce.9
  206.4 61.2 reduce-scatter.1
